TPU v7x, 256 devices: a whole 4x4x8 slice. The times are simulated.
256 devices in a mesh: seq: 32 (over z, y), mp: 8 (over x, core).
Axes of the slice: x: 4, y: 4, z: 8, core: 2. Of those that a mesh axis runs over, the one named last changes fastest.
Arguments:
- tokens: bfloat16 [12288, 4096], P('seq', 'mp'), may hold values from -6 to 6
- norm_gain: float32 [2, 4096], replicated, may hold values from 0.25 to 1.75
- in_weight: bfloat16 [2, 3, 4096, 4096], P(None, None, 'seq', 'mp'), may hold values from -0.09375 to 0.09375
- feat_filter: float32 [2, 3, 3, 4096], P(None, None, None, 'mp'), may hold values from -3 to 3
- short_filter: float32 [256, 7], P('mp'), may hold values from -3 to 3
- medium_filter: float32 [256, 128], P('mp'), may hold values from -0.4 to 0.4
- out_weight: bfloat16 [4096, 4096], P('seq', 'mp'), may hold values from -0.09375 to 0.09375
Outputs:
- stream: bfloat16 [12288, 4096], P('seq', 'mp')
- mixed: bfloat16 [12288, 4096], P('seq', 'mp')
All inputs are finite; a program needn't handle non-finite values.
Results may differ from a plain program's by a relative error of at most 0.015.
Values may be sent and summed in bfloat16 or wider, within the bound.
A program may use at most 128 MiB of HBM per device.

v0:
```python
import jax
import jax.numpy as jnp
from jax import lax
from jax.sharding import PartitionSpec as P


def shifted(x, axis, by):
    peers = lax.axis_size(axis)
    pairs = [(i, i + by) for i in range(peers) if 0 <= i + by < peers]
    return lax.ppermute(x, axis, pairs)


def causal_taps(extended, taps, count):
    reach = taps.shape[0] - 1
    offset = extended.shape[0] - count - reach
    values = extended.astype(jnp.float32)
    total = jnp.zeros((count, extended.shape[1]), jnp.float32)
    for index in range(reach + 1):
        begin = offset + reach - index
        total = total + taps[index] * values[begin : begin + count]
    return total


def toeplitz_conv(kv_ext, filt, count):
    width = filt.shape[1]
    channels = kv_ext.shape[1]
    groups_here = filt.shape[0]
    per_group = channels // groups_here
    padded = jnp.concatenate([jnp.zeros((1, channels), kv_ext.dtype), kv_ext], axis=0)
    blocks = padded.astype(jnp.float32).reshape(count // width + 1, width, groups_here, per_group)
    lag = jnp.arange(width)[:, None] - jnp.arange(width)[None, :]
    current = jnp.where(lag >= 0, filt[:, jnp.clip(lag, 0, width - 1)], 0.0)
    earlier = jnp.where(lag < 0, filt[:, jnp.clip(lag + width, 0, width - 1)], 0.0)
    out = jnp.einsum("gik,bkgc->bigc", current, blocks[1:], precision=lax.Precision.HIGHEST)
    out = out + jnp.einsum("gik,bkgc->bigc", earlier, blocks[:-1], precision=lax.Precision.HIGHEST)
    return out.reshape(count, channels)


def normalized(stream_loc, gain):
    full = lax.all_gather(stream_loc, "mp", axis=1, tiled=True)
    values = full.astype(jnp.float32)
    mean_sq = jnp.mean(values * values, axis=-1, keepdims=True)
    return (values * lax.rsqrt(mean_sq + 1e-06) * gain).astype(jnp.bfloat16)


def project(normed, weights):
    return jnp.einsum(
        "rd,cdf->crf",
        normed,
        lax.all_gather(weights, "seq", axis=1, tiled=True),
        preferred_element_type=jnp.float32,
    ).astype(jnp.bfloat16)


def gated_mix(proj, feat_taps, inner_fn, span):
    rows = proj.shape[1]
    reach = feat_taps.shape[1] - 1
    rim = shifted(proj[:, rows - reach :, :], "seq", 1)
    extended = jnp.concatenate([rim, proj], axis=1)
    query = causal_taps(extended[0], feat_taps[0], rows)
    key_part = causal_taps(extended[1], feat_taps[1], rows)
    value_part = causal_taps(extended[2], feat_taps[2], rows)
    kv_prod = (key_part * value_part).astype(jnp.bfloat16)
    earlier = shifted(kv_prod[rows - span :], "seq", 1)
    kv_ext = jnp.concatenate([earlier, kv_prod], axis=0)
    inner = inner_fn(kv_ext, rows)
    return (query * inner).astype(jnp.bfloat16)


def local(tokens, norm_gain, in_weight, feat_filter, short_filter, medium_filter, out_weight):
    per_group = tokens.shape[1] // short_filter.shape[0]
    short_taps = jnp.repeat(short_filter.T, per_group, axis=1)

    def short_inner(kv_ext, count):
        return causal_taps(kv_ext, short_taps, count)

    def medium_inner(kv_ext, count):
        return toeplitz_conv(kv_ext, medium_filter, count)

    normed = normalized(tokens, norm_gain[0])
    proj = project(normed, in_weight[0])
    first = gated_mix(proj, feat_filter[0], short_inner, short_filter.shape[1] - 1)
    first_full = lax.all_gather(first, "mp", axis=1, tiled=True)
    delta = jnp.dot(
        first_full,
        lax.all_gather(out_weight, "seq", axis=0, tiled=True),
        preferred_element_type=jnp.float32,
    )
    stream = (tokens.astype(jnp.float32) + delta).astype(jnp.bfloat16)
    normed_next = normalized(stream, norm_gain[1])
    proj_next = project(normed_next, in_weight[1])
    mixed = gated_mix(proj_next, feat_filter[1], medium_inner, medium_filter.shape[1] - 1)
    return (stream, mixed)


def solution(mesh):
    placed = (
        P("seq", "mp"),
        P(),
        P(None, None, "seq", "mp"),
        P(None, None, None, "mp"),
        P("mp", None),
        P("mp", None),
        P("seq", "mp"),
    )
    return jax.shard_map(
        local,
        mesh=mesh,
        in_specs=placed,
        out_specs=(P("seq", "mp"), P("seq", "mp")),
        check_vma=False,
    )
```

profile of v0, /device:TPU:88, one launch (start us, length us, event | category | flops | bytes accessed | tf_op | source)
XLA Modules:
  0.0 597.8 jit_solution(11730328731184018714)
XLA Ops:
  7.9 2.1 fusion.119
  11.7 30.4 %all-gather.9.cloned.1.call-done = bf16[384,4096]{1,0:T(8,128)(2,1)} async-done(((bf16[384,512]{1,0:T(8,128)(2,1)}), bf16[384,4096]{1,0:T(8,128)(2,1)}) %all-gather.9.cloned.1.call-update) | async-done | bytes 3145744 | tf_op jit(solution)/shard_map/all_gather | solution.py:40
  42.1 2.7 fusion.4
  44.9 116.5 %all-gather.17.cloned.1.call-done = bf16[1,3,4096,512]{3,2,1,0:T(8,128)(2,1)} async-done(((bf16[1,3,128,512]{3,2,1,0:T(8,128)(2,1)}), bf16[1,3,4096,512]{3,2,1,0:T(8,128)(2,1)}) %all-gather.17.cloned.1.call-update) | async-done | bytes 12582928 | tf_op jit(solution)/shard_map/all_gather | solution.py:50
  161.4 8.3 %fusion.39 = bf16[3,384,512]{2,1,0:T(8,128)(2,1)S(1)} fusion(bf16[1,3,4096,512]{3,2,1,0:T(8,128)(2,1)} %all-gather.17.cloned.1.call-done, bf16[384,4096]{1,0:T(8,128)(2,1)S(1)} %copy-done.1, f32[4096]{0:T(1024)S(1)} %bitcast.255, f32[384]{0:T(512)S(1)} %add_rsqrt_fusion.1), kind=kOutput, calls=%fused_computation.35 | convolution fusion | flops 4838719488 | bytes 16926208 | tf_op jit(solution)/shard_map/rd,cdf->crf/dot_general | solution.py:47
  169.7 6.5 %collective-permute-start = (bf16[3,2,512]{2,1,0:T(2,128)(2,1)S(1)}, bf16[3,2,512]{2,1,0:T(2,128)(2,1)S(1)}, u32[]{:S(2)}, u32[]{:S(2)}) collective-permute-start(bf16[3,2,512]{2,1,0:T(2,128)(2,1)S(1)} %slice.436), channel_id=1, source_target_pairs={{0,8},{8,16},{16,24},{24,32},{32,40},{40,48},{48,56},{56,64},{64,7... | collective-permute-start | bytes 18440 | tf_op jit(solution)/shard_map/ppermute | solution.py:10
  178.3 6.3 %collective-permute-start.1 = (bf16[6,512]{1,0:T(8,128)(2,1)S(1)}, bf16[6,512]{1,0:T(8,128)(2,1)S(1)}, u32[]{:S(2)}, u32[]{:S(2)}) collective-permute-start(bf16[6,512]{1,0:T(8,128)(2,1)S(1)} %slice.450), channel_id=1, source_target_pairs={{0,8},{8,16},{16,24},{24,32},{32,40},{40,48},{48,56},{56,64},{64,7... | collective-permute-start | bytes 18440 | tf_op jit(solution)/shard_map/ppermute | solution.py:10
  187.9 55.7 %all-gather.13.cloned.1.call-done = bf16[4096,512]{1,0:T(8,128)(2,1)} async-done(((bf16[128,512]{1,0:T(8,128)(2,1)}), bf16[4096,512]{1,0:T(8,128)(2,1)}) %all-gather.13.cloned.1.call-update) | async-done | bytes 4194320 | tf_op jit(solution)/shard_map/all_gather | solution.py:86
  243.6 32.9 %all-gather.11.cloned.1.call-done = bf16[384,4096]{1,0:T(8,128)(2,1)} async-done(((bf16[384,512]{1,0:T(8,128)(2,1)}), bf16[384,4096]{1,0:T(8,128)(2,1)}) %all-gather.11.cloned.1.call-update) | async-done | bytes 3145744 | tf_op jit(solution)/shard_map/all_gather | solution.py:83
  276.5 5.7 fusion.50
  282.8 29.9 %all-gather.15.cloned.1.call-done = bf16[384,4096]{1,0:T(8,128)(2,1)} async-done(((bf16[384,512]{1,0:T(8,128)(2,1)}), bf16[384,4096]{1,0:T(8,128)(2,1)}) %all-gather.15.cloned.1.call-update) | async-done | bytes 3145744 | tf_op jit(solution)/shard_map/all_gather | solution.py:40
  312.7 2.7 fusion.7
  315.4 116.4 %all-gather.19.cloned.1.call-done = bf16[1,3,4096,512]{3,2,1,0:T(8,128)(2,1)} async-done(((bf16[1,3,128,512]{3,2,1,0:T(8,128)(2,1)}), bf16[1,3,4096,512]{3,2,1,0:T(8,128)(2,1)}) %all-gather.19.cloned.1.call-update) | async-done | bytes 12582928 | tf_op jit(solution)/shard_map/all_gather | solution.py:50
  431.8 8.2 %fusion.34 = bf16[3,384,512]{2,1,0:T(8,128)(2,1)S(1)} fusion(bf16[1,3,4096,512]{3,2,1,0:T(8,128)(2,1)} %all-gather.19.cloned.1.call-done, bf16[384,4096]{1,0:T(8,128)(2,1)S(1)} %copy-done.2, f32[4096]{0:T(1024)S(1)} %bitcast.254, f32[384]{0:T(512)S(1)} %add_rsqrt_fusion), kind=kOutput, calls=%fused_computation.34 | convolution fusion | flops 4838719488 | bytes 16926208 | tf_op jit(solution)/shard_map/rd,cdf->crf/dot_general | solution.py:47
  440.1 6.5 %collective-permute-start.2 = (bf16[3,2,512]{2,1,0:T(2,128)(2,1)S(1)}, bf16[3,2,512]{2,1,0:T(2,128)(2,1)S(1)}, u32[]{:S(2)}, u32[]{:S(2)}) collective-permute-start(bf16[3,2,512]{2,1,0:T(2,128)(2,1)S(1)} %slice.458), channel_id=1, source_target_pairs={{0,8},{8,16},{16,24},{24,32},{32,40},{40,48},{48,56},{56,64},{64,7... | collective-permute-start | bytes 18440 | tf_op jit(solution)/shard_map/ppermute | solution.py:10
  448.8 6.5 %collective-permute-start.3 = (bf16[127,512]{1,0:T(8,128)(2,1)S(1)}, bf16[127,512]{1,0:T(8,128)(2,1)}, u32[]{:S(2)}, u32[]{:S(2)}) collective-permute-start(bf16[127,512]{1,0:T(8,128)(2,1)S(1)} %slice.472), channel_id=1, source_target_pairs={{0,8},{8,16},{16,24},{24,32},{32,40},{40,48},{48,56},{56,64},{64,7... | collective-permute-start | bytes 390152 | tf_op jit(solution)/shard_map/ppermute | solution.py:10
  456.0 54.8 %gather_fusion.1 = f32[16384,32]{1,0:T(8,128)} fusion(f32[32,128]{0,1:T(8,128)S(1)} %copy.17, s32[16384]{0:T(1024)S(1)} %fusion.114), kind=kCustom, calls=%fused_computation.1 | custom fusion | bytes 4259840 | tf_op jit(solution)/shard_map/gather | solution.py:33
  510.8 5.5 copy.22
  516.3 54.8 %gather_fusion = f32[16384,32]{1,0:T(8,128)} fusion(f32[32,128]{0,1:T(8,128)S(1)} %copy.17, s32[16384]{0:T(1024)S(1)} %fusion.112), kind=kCustom, calls=%fused_computation | custom fusion | bytes 4259840 | tf_op jit(solution)/shard_map/gather | solution.py:32
  571.1 6.4 %copy.18 = f32[128,128,32]{1,0,2:T(8,128)} copy(f32[128,128,32]{2,1,0:T(8,128)} %bitcast.250) | data formatting | bytes 4194304 | tf_op jit(solution)/shard_map/gather | solution.py:32
  578.4 2.0 slice.428
  580.5 1.8 pad_maximum_fusion.2
  584.4 2.9 fusion.18
  587.4 1.8 fusion.47
  (82 shorter events, 16.0 us)
Async XLA Ops:
  7.2 35.0 %all-gather.9.cloned.1.call-start = ((), (), s32[]{:S(2)}) async-start(), calls=%async_computation | async-start | bytes 3538944 | tf_op jit(solution)/shard_map/all_gather | solution.py:40
  7.9 153.5 %all-gather.17.cloned.1.call-start = ((), (), s32[]{:S(2)}) async-start(), calls=%async_computation.4 | async-start | bytes 12976128 | tf_op jit(solution)/shard_map/all_gather | solution.py:50
  10.0 233.5 %all-gather.13.cloned.1.call-start = ((), (), s32[]{:S(2)}) async-start(), calls=%async_computation.2 | async-start | bytes 4325376 | tf_op jit(solution)/shard_map/all_gather | solution.py:86
  10.8 265.7 %all-gather.11.cloned.1.call-start = ((), (), s32[]{:S(2)}) async-start(), calls=%async_computation.1 | async-start | bytes 3538944 | tf_op jit(solution)/shard_map/all_gather | solution.py:83
  42.1 119.3 %copy-start.1 = (bf16[384,4096]{1,0:T(8,128)(2,1)S(1)}, bf16[384,4096]{1,0:T(8,128)(2,1)}, u32[]{:S(2)}) copy-start(bf16[384,4096]{1,0:T(8,128)(2,1)} %all-gather.9.cloned.1.call-done) | copy-start | bytes 9437188
  161.4 14.8 %copy-start.6 = (f32[2,3,3,512]{3,0,2,1:T(2,128)S(1)}, f32[2,3,3,512]{3,0,2,1:T(2,128)}, u32[]{:S(2)}) copy-start(f32[2,3,3,512]{3,0,2,1:T(2,128)} %param.10) | copy-start | bytes 110596
  169.7 7.8 %collective-permute-start = (bf16[3,2,512]{2,1,0:T(2,128)(2,1)S(1)}, bf16[3,2,512]{2,1,0:T(2,128)(2,1)S(1)}, u32[]{:S(2)}, u32[]{:S(2)}) collective-permute-start(bf16[3,2,512]{2,1,0:T(2,128)(2,1)S(1)} %slice.436), channel_id=1, source_target_pairs={{0,8},{8,16},{16,24},{24,32},{32,40},{40,48},{48,56},{56,64},{64,7... | collective-permute-start | bytes 18440 | tf_op jit(solution)/shard_map/ppermute | solution.py:10
  177.8 6.8 %copy-start.11 = (f32[32,7]{0,1:T(8,128)S(1)}, f32[32,7]{0,1:T(8,128)}, u32[]{:S(2)}) copy-start(f32[32,7]{0,1:T(8,128)} %param.11) | copy-start | bytes 2692
  178.3 7.7 %collective-permute-start.1 = (bf16[6,512]{1,0:T(8,128)(2,1)S(1)}, bf16[6,512]{1,0:T(8,128)(2,1)S(1)}, u32[]{:S(2)}, u32[]{:S(2)}) collective-permute-start(bf16[6,512]{1,0:T(8,128)(2,1)S(1)} %slice.450), channel_id=1, source_target_pairs={{0,8},{8,16},{16,24},{24,32},{32,40},{40,48},{48,56},{56,64},{64,7... | collective-permute-start | bytes 18440 | tf_op jit(solution)/shard_map/ppermute | solution.py:10
  186.1 90.3 %copy-start.4 = (bf16[384,512]{1,0:T(8,128)(2,1)S(1)}, bf16[384,512]{1,0:T(8,128)(2,1)}, u32[]{:S(2)}) copy-start(bf16[384,512]{1,0:T(8,128)(2,1)} %param.7) | copy-start | bytes 1179652
  187.8 124.9 %all-gather.15.cloned.1.call-start = ((), (), s32[]{:S(2)}) async-start(), calls=%async_computation.3 | async-start | bytes 3538944 | tf_op jit(solution)/shard_map/all_gather | solution.py:40
  282.2 149.6 %all-gather.19.cloned.1.call-start = ((), (), s32[]{:S(2)}) async-start(), calls=%async_computation.5 | async-start | bytes 12976128 | tf_op jit(solution)/shard_map/all_gather | solution.py:50
  312.7 119.1 %copy-start.2 = (bf16[384,4096]{1,0:T(8,128)(2,1)S(1)}, bf16[384,4096]{1,0:T(8,128)(2,1)}, u32[]{:S(2)}) copy-start(bf16[384,4096]{1,0:T(8,128)(2,1)} %all-gather.15.cloned.1.call-done) | copy-start | bytes 9437188
  440.1 7.8 %collective-permute-start.2 = (bf16[3,2,512]{2,1,0:T(2,128)(2,1)S(1)}, bf16[3,2,512]{2,1,0:T(2,128)(2,1)S(1)}, u32[]{:S(2)}, u32[]{:S(2)}) collective-permute-start(bf16[3,2,512]{2,1,0:T(2,128)(2,1)S(1)} %slice.458), channel_id=1, source_target_pairs={{0,8},{8,16},{16,24},{24,32},{32,40},{40,48},{48,56},{56,64},{64,7... | collective-permute-start | bytes 18440 | tf_op jit(solution)/shard_map/ppermute | solution.py:10
  448.2 7.7 %copy-start.7 = (f32[32,128]{1,0:T(8,128)S(1)}, f32[32,128]{1,0:T(8,128)}, u32[]{:S(2)}) copy-start(f32[32,128]{1,0:T(8,128)} %param.12) | copy-start | bytes 49156
  448.8 131.7 %collective-permute-start.3 = (bf16[127,512]{1,0:T(8,128)(2,1)S(1)}, bf16[127,512]{1,0:T(8,128)(2,1)}, u32[]{:S(2)}, u32[]{:S(2)}) collective-permute-start(bf16[127,512]{1,0:T(8,128)(2,1)S(1)} %slice.472), channel_id=1, source_target_pairs={{0,8},{8,16},{16,24},{24,32},{32,40},{40,48},{48,56},{56,64},{64,7... | collective-permute-start | bytes 390152 | tf_op jit(solution)/shard_map/ppermute | solution.py:10
  577.5 6.9 %copy-start.5 = (pred[128,128]{1,0:T(8,128)(4,1)S(1)}, pred[128,128]{1,0:T(8,128)(4,1)}, u32[]{:S(2)}) copy-start(pred[128,128]{1,0:T(8,128)(4,1)} %fusion.115) | copy-start | bytes 49156
  584.4 3.0 copy-start
  584.4 3.0 copy-start.3
  589.1 0.8 copy-start.8
  589.1 0.8 copy-start.9
  589.1 0.8 copy-start.10
Sparse Core Ops, SparseCore 0:
  9.8 32.2 all-gather.8
  45.3 116.0 all-gather.16
  164.0 79.5 all-gather.12
  245.8 30.5 all-gather.10
  282.3 30.3 all-gather.14
  315.7 116.0 all-gather.18
where the time goes:
time: 598 us
  waiting for transfers between devices  386 us (65%)
  local copies, waits for them, and re-layouts  132 us (22%)
  matrix products  26.9 us (4%)
  starting transfers between devices  26 us (4%)
  between operations  14.4 us (2%)
  other arithmetic  12.3 us (2%)
    all_gather x2, waiting for transfers between devices, project(): lax.all_gather(weights, 'seq', axis=1, tiled=True)  233 us
    gather x2, local copies, waits for them, and re-layouts, toeplitz_conv(): current = jnp.where(lag >= 0, filt[:, jnp.clip(lag, 0, width - 1)], 0.0)  61.2 us
    all_gather x2, waiting for transfers between devices, normalized(): full = lax.all_gather(stream_loc, 'mp', axis=1, tiled=True)  60.3 us
    gather x2, local copies, waits for them, and re-layouts, toeplitz_conv(): filt[:, jnp.clip(lag + width, 0, width - 1)]  60.3 us
    all_gather x1, waiting for transfers between devices, local(): lax.all_gather(out_weight, 'seq', axis=0, tiled=True)  55.7 us
    all_gather x1, waiting for transfers between devices, local(): first_full = lax.all_gather(first, 'mp', axis=1, tiled=True)  32.9 us
    ppermute x4, starting transfers between devices, shifted(): return lax.ppermute(x, axis, pairs)  25.8 us
    dot_general x2, matrix products, project(): jnp.einsum('rd,cdf->crf', normed, lax.all_gather(weights, 'seq', axis=1,...  16.5 us
  transfers between devices with their start and end apart: 10, of which 9 were waited for; matrix products, arithmetic and copies ran while one was open for 24% of the time, Pallas kernels for 0%

commit v1 on v0

--- a/solution.py
+++ b/solution.py
@@ -37,7 +37,18 @@
 
 
 def normalized(stream_loc, gain):
-    full = lax.all_gather(stream_loc, "mp", axis=1, tiled=True)
+    degree = lax.axis_size("mp")
+    buffer = tuple(((d, (d + 1) % degree) for d in range(degree)))
+    main, long_array = ([stream_loc], [stream_loc])
+    slots = tuple(((d, (d - 1) % degree) for d in range(degree)))
+    for _ in range(degree // 2):
+        main.append(lax.ppermute(main[-1], "mp", buffer))
+    t = 0
+    while t < (degree - 1) // 2:
+        long_array.append(lax.ppermute(long_array[-1], "mp", slots))
+        t = t + 1
+    block_out = jnp.concatenate([*main[::-1], *long_array[1:]], axis=1)
+    full = jnp.roll(block_out, (lax.axis_index("mp") - degree // 2) * stream_loc.shape[1], axis=1)
     values = full.astype(jnp.float32)
     mean_sq = jnp.mean(values * values, axis=-1, keepdims=True)
     return (values * lax.rsqrt(mean_sq + 1e-06) * gain).astype(jnp.bfloat16)

time: 598 us -> 531 us (0.89)
  waiting for transfers between devices: 386 us -> 291 us
  starting transfers between devices: 26 us -> 44.7 us
  local copies, waits for them, and re-layouts: 132 us -> 140 us
    all_gather x2, waiting for transfers between devices: 233 us -> 154 us  [project(): lax.all_gather(weights, 'seq', axis=1, tiled=True)]
    all_gather x2 -> x0, waiting for transfers between devices: 60.3 us -> none  [normalized(): full = lax.all_gather(stream_loc, 'mp', axis=1, tiled=True)]
    ppermute x0 -> x14, waiting for transfers between devices: none -> 47.6 us  [the longest x8 47.5 us: normalized(): main.append(lax.ppermute(main[-1], 'mp', buffer))]
    ppermute x0 -> x14, starting transfers between devices: none -> 18.5 us  [the longest x6 18.2 us: normalized(): long_array.append(lax.ppermute(long_array[-1], 'mp', slots))]
    unnamed x26 -> x58, local copies, waits for them, and re-layouts: 0.22 us -> 6.64 us
  transfers between devices with their start and end apart: 10 -> 22, of which waited for: 9 -> 16; matrix products, arithmetic and copies ran while one was open for 24% -> 29% of each run, Pallas kernels for 0% -> 0%
where the time goes in v1:
time: 531 us; the launch traced here: 530 us
  waiting for transfers between devices  291 us (55%)
  local copies, waits for them, and re-layouts  140 us (26%)
  starting transfers between devices  44.7 us (8%)
  matrix products  28.2 us (5%)
  between operations  14.4 us (3%)
  other arithmetic  11.5 us (2%)
    all_gather x2, waiting for transfers between devices, project(): lax.all_gather(weights, 'seq', axis=1, tiled=True)  154 us
    gather x2, local copies, waits for them, and re-layouts, toeplitz_conv(): current = jnp.where(lag >= 0, filt[:, jnp.clip(lag, 0, width - 1)], 0.0)  60.9 us
    gather x2, local copies, waits for them, and re-layouts, toeplitz_conv(): filt[:, jnp.clip(lag + width, 0, width - 1)]  59.9 us
    all_gather x1, waiting for transfers between devices, local(): lax.all_gather(out_weight, 'seq', axis=0, tiled=True)  53.5 us
    ppermute x8, waiting for transfers between devices, normalized(): main.append(lax.ppermute(main[-1], 'mp', buffer))  47.5 us
    all_gather x1, waiting for transfers between devices, local(): first_full = lax.all_gather(first, 'mp', axis=1, tiled=True)  33 us
    ppermute x4, starting transfers between devices, shifted(): return lax.ppermute(x, axis, pairs)  25.8 us
    dot_general x2, matrix products, project(): jnp.einsum('rd,cdf->crf', normed, lax.all_gather(weights, 'seq', axis=1,...  19.8 us
  transfers between devices with their start and end apart: 22, of which 16 were waited for; matrix products, arithmetic and copies ran while one was open for 29% of the time, Pallas kernels for 0%

profile of v1, /device:TPU:88, one launch (start us, length us, event | category | flops | bytes accessed | tf_op | source)
XLA Modules:
  0.0 530.3 jit_solution(18371910110335068892)
XLA Ops:
  10.2 8.6 %collective-permute-done = bf16[384,512]{1,0:T(8,128)(2,1)S(1)} collective-permute-done((bf16[384,512]{1,0:T(8,128)(2,1)}, bf16[384,512]{1,0:T(8,128)(2,1)S(1)}, u32[]{:S(2)}, u32[]{:S(2)}) %collective-permute-start) | collective-permute-done | bytes 393248 | tf_op jit(solution)/shard_map/ppermute | solution.py:45
  22.5 5.5 %collective-permute-done.1 = bf16[384,512]{1,0:T(8,128)(2,1)S(1)} collective-permute-done((bf16[384,512]{1,0:T(8,128)(2,1)S(1)}, bf16[384,512]{1,0:T(8,128)(2,1)S(1)}, u32[]{:S(2)}, u32[]{:S(2)}) %collective-permute-start.1) | collective-permute-done | bytes 393248 | tf_op jit(solution)/shard_map/ppermute | solution.py:45
  28.1 3.4 collective-permute-start.5
  31.5 4.8 collective-permute-done.2
  40.8 4.1 collective-permute-done.3
  53.3 75.9 %all-gather.11.cloned.1.call-done = bf16[1,3,4096,512]{3,2,1,0:T(8,128)(2,1)} async-done(((bf16[1,3,128,512]{3,2,1,0:T(8,128)(2,1)}), bf16[1,3,4096,512]{3,2,1,0:T(8,128)(2,1)}) %all-gather.11.cloned.1.call-update) | async-done | bytes 12582928 | tf_op jit(solution)/shard_map/all_gather | solution.py:61
  129.2 9.9 %fusion.41 = bf16[3,384,512]{2,1,0:T(8,128)(2,1)S(1)} fusion(bf16[1,3,4096,512]{3,2,1,0:T(8,128)(2,1)} %all-gather.11.cloned.1.call-done, f32[4096]{0:T(1024)} %bitcast.255, f32[384]{0:T(512)} %add_rsqrt_fusion.1, s32[]{:T(128)S(6)} %select_n.46, bf16[384,4096]{1,0:T(8,128)(2,1)S(1)} %constant_dynamic-update-slice_fusion), kind=kOutput, calls=%fused_computation.41 | convolution fusion | flops 4843438080 | bytes 16926212 | tf_op jit(solution)/shard_map/rd,cdf->crf/dot_general | solution.py:58
  139.1 6.5 %collective-permute-start.7 = (bf16[3,2,512]{2,1,0:T(2,128)(2,1)S(1)}, bf16[3,2,512]{2,1,0:T(2,128)(2,1)S(1)}, u32[]{:S(2)}, u32[]{:S(2)}) collective-permute-start(bf16[3,2,512]{2,1,0:T(2,128)(2,1)S(1)} %slice.436), channel_id=1, source_target_pairs={{0,8},{8,16},{16,24},{24,32},{32,40},{40,48},{48,56},{56,64},{64,7... | collective-permute-start | bytes 18440 | tf_op jit(solution)/shard_map/ppermute | solution.py:10
  147.8 6.3 %collective-permute-start.8 = (bf16[6,512]{1,0:T(8,128)(2,1)S(1)}, bf16[6,512]{1,0:T(8,128)(2,1)S(1)}, u32[]{:S(2)}, u32[]{:S(2)}) collective-permute-start(bf16[6,512]{1,0:T(8,128)(2,1)S(1)} %slice.450), channel_id=1, source_target_pairs={{0,8},{8,16},{16,24},{24,32},{32,40},{40,48},{48,56},{56,64},{64,7... | collective-permute-start | bytes 18440 | tf_op jit(solution)/shard_map/ppermute | solution.py:10
  157.8 53.5 %all-gather.9.cloned.1.call-done = bf16[4096,512]{1,0:T(8,128)(2,1)} async-done(((bf16[128,512]{1,0:T(8,128)(2,1)}), bf16[4096,512]{1,0:T(8,128)(2,1)}) %all-gather.9.cloned.1.call-update) | async-done | bytes 4194320 | tf_op jit(solution)/shard_map/all_gather | solution.py:97
  211.3 33.0 %all-gather.7.cloned.1.call-done = bf16[384,4096]{1,0:T(8,128)(2,1)} async-done(((bf16[384,512]{1,0:T(8,128)(2,1)}), bf16[384,4096]{1,0:T(8,128)(2,1)}) %all-gather.7.cloned.1.call-update) | async-done | bytes 3145744 | tf_op jit(solution)/shard_map/all_gather | solution.py:94
  244.4 4.9 fusion.52
  249.6 8.2 %collective-permute-done.9 = bf16[384,512]{1,0:T(8,128)(2,1)S(1)} collective-permute-done((bf16[384,512]{1,0:T(8,128)(2,1)S(1)}, bf16[384,512]{1,0:T(8,128)(2,1)S(1)}, u32[]{:S(2)}, u32[]{:S(2)}) %collective-permute-start.9) | collective-permute-done | bytes 393248 | tf_op jit(solution)/shard_map/ppermute | solution.py:45
  260.7 5.5 %collective-permute-done.10 = bf16[384,512]{1,0:T(8,128)(2,1)S(1)} collective-permute-done((bf16[384,512]{1,0:T(8,128)(2,1)S(1)}, bf16[384,512]{1,0:T(8,128)(2,1)S(1)}, u32[]{:S(2)}, u32[]{:S(2)}) %collective-permute-start.10) | collective-permute-done | bytes 393248 | tf_op jit(solution)/shard_map/ppermute | solution.py:45
  269.1 5.5 %collective-permute-done.11 = bf16[384,512]{1,0:T(8,128)(2,1)S(1)} collective-permute-done((bf16[384,512]{1,0:T(8,128)(2,1)S(1)}, bf16[384,512]{1,0:T(8,128)(2,1)S(1)}, u32[]{:S(2)}, u32[]{:S(2)}) %collective-permute-start.11) | collective-permute-done | bytes 393248 | tf_op jit(solution)/shard_map/ppermute | solution.py:45
  277.6 5.4 %collective-permute-done.12 = bf16[384,512]{1,0:T(8,128)(2,1)S(1)} collective-permute-done((bf16[384,512]{1,0:T(8,128)(2,1)S(1)}, bf16[384,512]{1,0:T(8,128)(2,1)S(1)}, u32[]{:S(2)}, u32[]{:S(2)}) %collective-permute-start.12) | collective-permute-done | bytes 393248 | tf_op jit(solution)/shard_map/ppermute | solution.py:45
  285.7 77.8 %all-gather.13.cloned.1.call-done = bf16[1,3,4096,512]{3,2,1,0:T(8,128)(2,1)} async-done(((bf16[1,3,128,512]{3,2,1,0:T(8,128)(2,1)}), bf16[1,3,4096,512]{3,2,1,0:T(8,128)(2,1)}) %all-gather.13.cloned.1.call-update) | async-done | bytes 12582928 | tf_op jit(solution)/shard_map/all_gather | solution.py:61
  363.5 9.9 %fusion.36 = bf16[3,384,512]{2,1,0:T(8,128)(2,1)S(1)} fusion(bf16[1,3,4096,512]{3,2,1,0:T(8,128)(2,1)} %all-gather.13.cloned.1.call-done, f32[4096]{0:T(1024)S(1)} %bitcast.254, f32[384]{0:T(512)S(1)} %add_rsqrt_fusion, s32[]{:T(128)S(6)} %select_n.46, bf16[384,4096]{1,0:T(8,128)(2,1)S(1)} %constant_dynamic-update-slice_fusion.8), kind=kOutput, calls=%fused_computation.40 | convolution fusion | flops 4843438080 | bytes 16926212 | tf_op jit(solution)/shard_map/rd,cdf->crf/dot_general | solution.py:58
  373.5 6.5 %collective-permute-start.16 = (bf16[3,2,512]{2,1,0:T(2,128)(2,1)S(1)}, bf16[3,2,512]{2,1,0:T(2,128)(2,1)S(1)}, u32[]{:S(2)}, u32[]{:S(2)}) collective-permute-start(bf16[3,2,512]{2,1,0:T(2,128)(2,1)S(1)} %slice.458), channel_id=1, source_target_pairs={{0,8},{8,16},{16,24},{24,32},{32,40},{40,48},{48,56},{56,64},{64,7... | collective-permute-start | bytes 18440 | tf_op jit(solution)/shard_map/ppermute | solution.py:10
  382.8 6.5 %collective-permute-start.17 = (bf16[127,512]{1,0:T(8,128)(2,1)}, bf16[127,512]{1,0:T(8,128)(2,1)}, u32[]{:S(2)}, u32[]{:S(2)}) collective-permute-start(bf16[127,512]{1,0:T(8,128)(2,1)} %slice.472), channel_id=1, source_target_pairs={{0,8},{8,16},{16,24},{24,32},{32,40},{40,48},{48,56},{56,64},{64,7... | collective-permute-start | bytes 390152 | tf_op jit(solution)/shard_map/ppermute | solution.py:10
  389.5 54.4 %gather_fusion.1 = f32[16384,32]{1,0:T(8,128)} fusion(f32[32,128]{0,1:T(8,128)S(1)} %copy.17, s32[16384]{0:T(1024)S(1)} %fusion.116), kind=kCustom, calls=%fused_computation.1 | custom fusion | bytes 4259840 | tf_op jit(solution)/shard_map/gather | solution.py:33
  443.9 5.5 %copy.22 = f32[128,128,32]{1,0,2:T(8,128)S(1)} copy(f32[128,128,32]{2,1,0:T(8,128)} %bitcast.251) | data formatting | bytes 4194304 | tf_op jit(solution)/shard_map/gather | solution.py:33
  449.4 54.4 %gather_fusion = f32[16384,32]{1,0:T(8,128)} fusion(f32[32,128]{0,1:T(8,128)S(1)} %copy.17, s32[16384]{0:T(1024)S(1)} %fusion.114), kind=kCustom, calls=%fused_computation | custom fusion | bytes 4259840 | tf_op jit(solution)/shard_map/gather | solution.py:32
  503.8 6.4 %copy.18 = f32[128,128,32]{1,0,2:T(8,128)} copy(f32[128,128,32]{2,1,0:T(8,128)} %bitcast.250) | data formatting | bytes 4194304 | tf_op jit(solution)/shard_map/gather | solution.py:32
  (138 shorter events, 53.5 us)
Async XLA Ops:
  7.2 42.0 %copy-start.2 = (bf16[384,512]{1,0:T(8,128)(2,1)S(1)}, bf16[384,512]{1,0:T(8,128)(2,1)}, u32[]{:S(2)}) copy-start(bf16[384,512]{1,0:T(8,128)(2,1)} %param.9) | copy-start | bytes 1179652
  7.2 122.0 %all-gather.11.cloned.1.call-start = ((), (), s32[]{:S(2)}) async-start(), calls=%async_computation.2 | async-start | bytes 12976128 | tf_op jit(solution)/shard_map/all_gather | solution.py:61
  9.4 202.0 %all-gather.9.cloned.1.call-start = ((), (), s32[]{:S(2)}) async-start(), calls=%async_computation.1 | async-start | bytes 4325376 | tf_op jit(solution)/shard_map/all_gather | solution.py:97
  10.1 234.3 %all-gather.7.cloned.1.call-start = ((), (), s32[]{:S(2)}) async-start(), calls=%async_computation | async-start | bytes 3538944 | tf_op jit(solution)/shard_map/all_gather | solution.py:94
  10.2 8.6 %collective-permute-start = (bf16[384,512]{1,0:T(8,128)(2,1)}, bf16[384,512]{1,0:T(8,128)(2,1)S(1)}, u32[]{:S(2)}, u32[]{:S(2)}) collective-permute-start(bf16[384,512]{1,0:T(8,128)(2,1)} %param.9), channel_id=1, source_target_pairs={{0,1},{1,2},{2,3},{3,4},{4,5},{5,6},{6,7},{7,0},{8,9},{9,10},{10,1... | collective-permute-start | bytes 1179656 | tf_op jit(solution)/shard_map/ppermute | solution.py:45
  19.5 8.4 %collective-permute-start.1 = (bf16[384,512]{1,0:T(8,128)(2,1)S(1)}, bf16[384,512]{1,0:T(8,128)(2,1)S(1)}, u32[]{:S(2)}, u32[]{:S(2)}) collective-permute-start(bf16[384,512]{1,0:T(8,128)(2,1)S(1)} %collective-permute-done), channel_id=1, source_target_pairs={{0,1},{1,2},{2,3},{3,4},{4,5},{5,6},{6,7},{7,0},{8,9},{9,10},{10,1... | collective-permute-start | bytes 1179656 | tf_op jit(solution)/shard_map/ppermute | solution.py:45
  19.5 8.6 %collective-permute-start.4 = (bf16[384,512]{1,0:T(8,128)(2,1)}, bf16[384,512]{1,0:T(8,128)(2,1)S(1)}, u32[]{:S(2)}, u32[]{:S(2)}) collective-permute-start(bf16[384,512]{1,0:T(8,128)(2,1)} %param.9), channel_id=1, source_target_pairs={{0,7},{1,0},{2,1},{3,2},{4,3},{5,4},{6,5},{7,6},{8,15},{9,8},{10,9... | collective-permute-start | bytes 1179656 | tf_op jit(solution)/shard_map/ppermute | solution.py:48
  28.0 8.4 %collective-permute-start.2 = (bf16[384,512]{1,0:T(8,128)(2,1)S(1)}, bf16[384,512]{1,0:T(8,128)(2,1)S(1)}, u32[]{:S(2)}, u32[]{:S(2)}) collective-permute-start(bf16[384,512]{1,0:T(8,128)(2,1)S(1)} %collective-permute-done.1), channel_id=1, source_target_pairs={{0,1},{1,2},{2,3},{3,4},{4,5},{5,6},{6,7},{7,0},{8,9},{9,10},{10,1... | collective-permute-start | bytes 1179656 | tf_op jit(solution)/shard_map/ppermute | solution.py:45
  28.1 9.7 %collective-permute-start.5 = (bf16[384,512]{1,0:T(8,128)(2,1)S(1)}, bf16[384,512]{1,0:T(8,128)(2,1)}, u32[]{:S(2)}, u32[]{:S(2)}) collective-permute-start(bf16[384,512]{1,0:T(8,128)(2,1)S(1)} %collective-permute-done.4), channel_id=1, source_target_pairs={{0,7},{1,0},{2,1},{3,2},{4,3},{5,4},{6,5},{7,6},{8,15},{9,8},{10,9... | collective-permute-start | bytes 1179656 | tf_op jit(solution)/shard_map/ppermute | solution.py:48
  36.4 8.5 %collective-permute-start.3 = (bf16[384,512]{1,0:T(8,128)(2,1)S(1)}, bf16[384,512]{1,0:T(8,128)(2,1)}, u32[]{:S(2)}, u32[]{:S(2)}) collective-permute-start(bf16[384,512]{1,0:T(8,128)(2,1)S(1)} %collective-permute-done.2), channel_id=1, source_target_pairs={{0,1},{1,2},{2,3},{3,4},{4,5},{5,6},{6,7},{7,0},{8,9},{9,10},{10,1... | collective-permute-start | bytes 1179656 | tf_op jit(solution)/shard_map/ppermute | solution.py:45
  37.8 12.5 %collective-permute-start.6 = (bf16[384,512]{1,0:T(8,128)(2,1)}, bf16[384,512]{1,0:T(8,128)(2,1)S(1)}, u32[]{:S(2)}, u32[]{:S(2)}) collective-permute-start(bf16[384,512]{1,0:T(8,128)(2,1)} %collective-permute-done.5), channel_id=1, source_target_pairs={{0,7},{1,0},{2,1},{3,2},{4,3},{5,4},{6,5},{7,6},{8,15},{9,8},{10,9... | collective-permute-start | bytes 1179656 | tf_op jit(solution)/shard_map/ppermute | solution.py:48
  139.1 7.8 %collective-permute-start.7 = (bf16[3,2,512]{2,1,0:T(2,128)(2,1)S(1)}, bf16[3,2,512]{2,1,0:T(2,128)(2,1)S(1)}, u32[]{:S(2)}, u32[]{:S(2)}) collective-permute-start(bf16[3,2,512]{2,1,0:T(2,128)(2,1)S(1)} %slice.436), channel_id=1, source_target_pairs={{0,8},{8,16},{16,24},{24,32},{32,40},{40,48},{48,56},{56,64},{64,7... | collective-permute-start | bytes 18440 | tf_op jit(solution)/shard_map/ppermute | solution.py:10
  147.8 7.7 %collective-permute-start.8 = (bf16[6,512]{1,0:T(8,128)(2,1)S(1)}, bf16[6,512]{1,0:T(8,128)(2,1)S(1)}, u32[]{:S(2)}, u32[]{:S(2)}) collective-permute-start(bf16[6,512]{1,0:T(8,128)(2,1)S(1)} %slice.450), channel_id=1, source_target_pairs={{0,8},{8,16},{16,24},{24,32},{32,40},{40,48},{48,56},{56,64},{64,7... | collective-permute-start | bytes 18440 | tf_op jit(solution)/shard_map/ppermute | solution.py:10
  157.3 206.2 %all-gather.13.cloned.1.call-start = ((), (), s32[]{:S(2)}) async-start(), calls=%async_computation.3 | async-start | bytes 12976128 | tf_op jit(solution)/shard_map/all_gather | solution.py:61
  249.3 34.0 %copy-start.3 = (bf16[384,512]{1,0:T(8,128)(2,1)}, bf16[384,512]{1,0:T(8,128)(2,1)S(1)}, u32[]{:S(2)}) copy-start(bf16[384,512]{1,0:T(8,128)(2,1)S(1)} %fusion.52) | copy-start | bytes 1179652
  249.3 8.4 %collective-permute-start.9 = (bf16[384,512]{1,0:T(8,128)(2,1)S(1)}, bf16[384,512]{1,0:T(8,128)(2,1)S(1)}, u32[]{:S(2)}, u32[]{:S(2)}) collective-permute-start(bf16[384,512]{1,0:T(8,128)(2,1)S(1)} %fusion.52), channel_id=1, source_target_pairs={{0,1},{1,2},{2,3},{3,4},{4,5},{5,6},{6,7},{7,0},{8,9},{9,10},{10,1... | collective-permute-start | bytes 1179656 | tf_op jit(solution)/shard_map/ppermute | solution.py:45
  257.7 8.4 %collective-permute-start.10 = (bf16[384,512]{1,0:T(8,128)(2,1)S(1)}, bf16[384,512]{1,0:T(8,128)(2,1)S(1)}, u32[]{:S(2)}, u32[]{:S(2)}) collective-permute-start(bf16[384,512]{1,0:T(8,128)(2,1)S(1)} %collective-permute-done.9), channel_id=1, source_target_pairs={{0,1},{1,2},{2,3},{3,4},{4,5},{5,6},{6,7},{7,0},{8,9},{9,10},{10,1... | collective-permute-start | bytes 1179656 | tf_op jit(solution)/shard_map/ppermute | solution.py:45
  257.7 8.4 %collective-permute-start.13 = (bf16[384,512]{1,0:T(8,128)(2,1)S(1)}, bf16[384,512]{1,0:T(8,128)(2,1)S(1)}, u32[]{:S(2)}, u32[]{:S(2)}) collective-permute-start(bf16[384,512]{1,0:T(8,128)(2,1)S(1)} %fusion.52), channel_id=1, source_target_pairs={{0,7},{1,0},{2,1},{3,2},{4,3},{5,4},{6,5},{7,6},{8,15},{9,8},{10,9... | collective-permute-start | bytes 1179656 | tf_op jit(solution)/shard_map/ppermute | solution.py:48
  266.2 8.4 %collective-permute-start.11 = (bf16[384,512]{1,0:T(8,128)(2,1)S(1)}, bf16[384,512]{1,0:T(8,128)(2,1)S(1)}, u32[]{:S(2)}, u32[]{:S(2)}) collective-permute-start(bf16[384,512]{1,0:T(8,128)(2,1)S(1)} %collective-permute-done.10), channel_id=1, source_target_pairs={{0,1},{1,2},{2,3},{3,4},{4,5},{5,6},{6,7},{7,0},{8,9},{9,10},{10,1... | collective-permute-start | bytes 1179656 | tf_op jit(solution)/shard_map/ppermute | solution.py:45
  266.2 8.4 %collective-permute-start.14 = (bf16[384,512]{1,0:T(8,128)(2,1)S(1)}, bf16[384,512]{1,0:T(8,128)(2,1)S(1)}, u32[]{:S(2)}, u32[]{:S(2)}) collective-permute-start(bf16[384,512]{1,0:T(8,128)(2,1)S(1)} %collective-permute-done.13), channel_id=1, source_target_pairs={{0,7},{1,0},{2,1},{3,2},{4,3},{5,4},{6,5},{7,6},{8,15},{9,8},{10,9... | collective-permute-start | bytes 1179656 | tf_op jit(solution)/shard_map/ppermute | solution.py:48
  274.6 8.4 %collective-permute-start.12 = (bf16[384,512]{1,0:T(8,128)(2,1)S(1)}, bf16[384,512]{1,0:T(8,128)(2,1)S(1)}, u32[]{:S(2)}, u32[]{:S(2)}) collective-permute-start(bf16[384,512]{1,0:T(8,128)(2,1)S(1)} %collective-permute-done.11), channel_id=1, source_target_pairs={{0,1},{1,2},{2,3},{3,4},{4,5},{5,6},{6,7},{7,0},{8,9},{9,10},{10,1... | collective-permute-start | bytes 1179656 | tf_op jit(solution)/shard_map/ppermute | solution.py:45
  274.6 8.7 %collective-permute-start.15 = (bf16[384,512]{1,0:T(8,128)(2,1)S(1)}, bf16[384,512]{1,0:T(8,128)(2,1)S(1)}, u32[]{:S(2)}, u32[]{:S(2)}) collective-permute-start(bf16[384,512]{1,0:T(8,128)(2,1)S(1)} %collective-permute-done.14), channel_id=1, source_target_pairs={{0,7},{1,0},{2,1},{3,2},{4,3},{5,4},{6,5},{7,6},{8,15},{9,8},{10,9... | collective-permute-start | bytes 1179656 | tf_op jit(solution)/shard_map/ppermute | solution.py:48
  373.5 7.8 %collective-permute-start.16 = (bf16[3,2,512]{2,1,0:T(2,128)(2,1)S(1)}, bf16[3,2,512]{2,1,0:T(2,128)(2,1)S(1)}, u32[]{:S(2)}, u32[]{:S(2)}) collective-permute-start(bf16[3,2,512]{2,1,0:T(2,128)(2,1)S(1)} %slice.458), channel_id=1, source_target_pairs={{0,8},{8,16},{16,24},{24,32},{32,40},{40,48},{48,56},{56,64},{64,7... | collective-permute-start | bytes 18440 | tf_op jit(solution)/shard_map/ppermute | solution.py:10
  382.8 130.4 %collective-permute-start.17 = (bf16[127,512]{1,0:T(8,128)(2,1)}, bf16[127,512]{1,0:T(8,128)(2,1)}, u32[]{:S(2)}, u32[]{:S(2)}) collective-permute-start(bf16[127,512]{1,0:T(8,128)(2,1)} %slice.472), channel_id=1, source_target_pairs={{0,8},{8,16},{16,24},{24,32},{32,40},{40,48},{48,56},{56,64},{64,7... | collective-permute-start | bytes 390152 | tf_op jit(solution)/shard_map/ppermute | solution.py:10
  (19 other events, 121.4 us)
Sparse Core Ops, SparseCore 0:
  11.2 117.9 all-gather.10
  131.8 79.5 all-gather.8
  213.8 30.5 all-gather.6
  247.4 116.0 all-gather.12
